TPU v7x, 32 devices: a whole 2x2x4 slice. The times are simulated.
32 devices in a mesh: fsdp: 8 (over y, x, core), sp: 4 (over z).
Axes of the slice: x: 2, y: 2, z: 4, core: 2. Of those that a mesh axis runs over, the one named last changes fastest.
Arguments:
- inputs: bfloat16 [32, 1024, 768], P('fsdp', 'sp'), may hold values from -6 to 6
- global_pos: int32 [32, 4], P('fsdp'), may hold values from 0 to 1023, as said below
- w_local: bfloat16 [3, 768, 768], P(None, 'fsdp'), may hold values from -0.21875 to 0.21875
- w_global: bfloat16 [3, 768, 768], P(None, 'fsdp'), may hold values from -0.3125 to 0.3125
- w_out: bfloat16 [768, 768], P('fsdp'), may hold values from -2.5 to 2.5
- b_proj: bfloat16 [6, 768], P(None, 'fsdp'), may hold values from -3 to 3
- gains: bfloat16 [2, 768], P(None, 'fsdp'), may hold values from 0.5 to 1.5
- shifts: bfloat16 [2, 768], P(None, 'fsdp'), may hold values from -3 to 3
- w_in: bfloat16 [768, 3072], P('fsdp'), may hold values from -0.21875 to 0.21875
- c_in: bfloat16 [3072], P('fsdp'), may hold values from -3 to 3
- w_back: bfloat16 [3072, 768], P('fsdp'), may hold values from -0.109375 to 0.109375
- cotangent: bfloat16 [32, 1024, 768], P('fsdp', 'sp'), may hold values from -6 to 6
Outputs:
- output: bfloat16 [32, 1024, 768], P('fsdp', 'sp')
- grad_inputs: bfloat16 [32, 1024, 768], P('fsdp', 'sp')
- grad_w_local: float32 [3, 768, 768], P(None, 'fsdp')
- grad_w_global: float32 [3, 768, 768], P(None, 'fsdp')
- grad_w_out: float32 [768, 768], P('fsdp')
- grad_b_proj: float32 [6, 768], P(None, 'fsdp')
- grad_gains: float32 [2, 768], P(None, 'fsdp')
- grad_shifts: float32 [2, 768], P(None, 'fsdp')
- grad_w_in: float32 [768, 3072], P('fsdp')
- grad_c_in: float32 [3072], P('fsdp')
- grad_w_back: float32 [3072, 768], P('fsdp')
Inputs may be any that keep to these rules, and one draw needn't show every extreme that they name: `global_pos`: in each sequence the 4 global positions are different; the first is 0 and the second is 1023.
All inputs are finite; a program needn't handle non-finite values.
Results may differ from a plain program's by a relative error of at most 0.017.
Values may be sent and summed in bfloat16 or wider, within the bound.
No kernel may reach another device: no remote copies, remote signals or barrier semaphores. Data moves between devices by JAX's collectives and lax.ppermute only.
A program may use at most 256 MiB of HBM per device.

v0:
```python
import jax
import jax.numpy as jnp
from jax import lax
from jax.sharding import PartitionSpec as P

HEADS = 12
HEAD_DIM = 64
WIN = 256
HIGHEST = lax.Precision.HIGHEST
MASKED_SCORE = -1000000000.0
NORM_EPS = 1e-05
BF = jnp.bfloat16
F32 = jnp.float32


def normalize(summed):
    center = summed - jnp.mean(summed, axis=-1, keepdims=True)
    inverse = lax.rsqrt(jnp.mean(center * center, axis=-1, keepdims=True) + NORM_EPS)
    return (center * inverse, inverse)


def norm_back(scaled, normed, inverse):
    return inverse * (
        scaled
        - jnp.mean(scaled, axis=-1, keepdims=True)
        - normed * jnp.mean(scaled * normed, axis=-1, keepdims=True)
    )


def mm(a, b):
    return jnp.dot(a, b, preferred_element_type=F32)


def mm_nt(a, b):
    return lax.dot_general(a, b, (((1,), (1,)), ((), ())), preferred_element_type=F32)


def mm_tn(a, b):
    return lax.dot_general(a, b, (((0,), (0,)), ((), ())), preferred_element_type=F32)


def gelu_pair(inner):
    cdf = 0.5 * (1.0 + lax.erf(inner * 0.5**0.5))
    pdf = jnp.exp(-0.5 * inner * inner) * 0.3989422804014327
    return (inner * cdf, cdf + inner * pdf)


def sequence_step(x, positions, upstream_low, weights):
    w_local, w_global, w_out, b_proj, gains, shifts, w_in, c_in, w_back = weights
    length, width = x.shape
    scale = HEAD_DIM ** (-0.5)
    bias = b_proj.astype(F32)
    gain = gains.astype(F32)
    shift = shifts.astype(F32)

    def heads(value):
        return value.reshape(value.shape[0], HEADS, HEAD_DIM)

    q = heads(((mm(x, w_local[0]) + bias[0]) * scale).astype(BF))
    k = heads(mm(x, w_local[1]).astype(BF))
    v = heads((mm(x, w_local[2]) + bias[1]).astype(BF))
    kg = heads(mm(x, w_global[1]).astype(BF))
    vg = heads((mm(x, w_global[2]) + bias[3]).astype(BF))
    places = jnp.arange(length, dtype=jnp.int32)
    select = positions[:, None] == places[None, :]
    select_low = select.astype(BF)
    select_full = select.astype(F32)
    is_glob = jnp.sum(select_full, axis=0)
    keep_local = 1.0 - is_glob
    rows_glob = mm(select_low, x).astype(BF)
    qg = heads(((mm(rows_glob, w_global[0]) + bias[2]) * scale).astype(BF))
    block = 256
    offsets = list(range(0, length, block))

    def block_scores(offset):
        qb = q[offset : offset + block]
        row_places = offset + jnp.arange(block, dtype=jnp.int32)
        in_band = jnp.abs(row_places[:, None] - places[None, :]) <= WIN
        allowed = in_band | (is_glob[None, :] > 0.5)
        raw = jnp.einsum("ihe,jhe->hij", qb, k, preferred_element_type=F32)
        return (qb, jnp.where(allowed[None], raw, MASKED_SCORE))

    kept = []
    contexts = []
    for offset in offsets:
        qb, masked = block_scores(offset)
        top = jnp.max(masked, axis=-1, keepdims=True)
        powers = jnp.exp(masked - top)
        total = jnp.sum(powers, axis=-1, keepdims=True)
        low = (powers / total).astype(BF)
        contexts.append(jnp.einsum("hij,jhe->ihe", low, v, preferred_element_type=F32))
        kept.append((top, total))
    context_loc = jnp.concatenate(contexts, axis=0)
    glob_scores = jnp.einsum("ghe,jhe->hgj", qg, kg, preferred_element_type=F32)
    glob_probs = jax.nn.softmax(glob_scores, axis=-1)
    glob_low = glob_probs.astype(BF)
    context_glob = jnp.einsum("hgj,jhe->ghe", glob_low, vg, preferred_element_type=F32)
    context = context_loc * keep_local[:, None, None] + jnp.einsum(
        "gl,ghe->lhe", select_full, context_glob, precision=HIGHEST
    )
    merged = context.astype(BF).reshape(length, width)
    attended = mm(merged, w_out) + bias[4]
    normed_one, inverse_one = normalize(x.astype(F32) + attended)
    first_norm = normed_one * gain[0] + shift[0]
    first_low = first_norm.astype(BF)
    inner = mm(first_low, w_in) + c_in.astype(F32)
    act, slope = gelu_pair(inner)
    active = act.astype(BF)
    normed_two, inverse_two = normalize(first_norm + (mm(active, w_back) + bias[5]))
    result = normed_two * gain[1] + shift[1]
    upstream = upstream_low.astype(F32)
    grad_gain_two = jnp.sum(upstream * normed_two, axis=0)
    grad_shift_two = jnp.sum(upstream, axis=0)
    grad_second = norm_back(upstream * gain[1], normed_two, inverse_two)
    branch_grad = grad_second.astype(BF)
    grad_back_w = mm_tn(active, branch_grad)
    grad_out_bias = jnp.sum(branch_grad.astype(F32), axis=0)
    inner_grad = (mm_nt(branch_grad, w_back) * slope).astype(BF)
    grad_in_w = mm_tn(first_low, inner_grad)
    grad_in_bias = jnp.sum(inner_grad.astype(F32), axis=0)
    grad_first = grad_second + mm_nt(inner_grad, w_in)
    grad_gain_one = jnp.sum(grad_first * normed_one, axis=0)
    grad_shift_one = jnp.sum(grad_first, axis=0)
    grad_sum_one = norm_back(grad_first * gain[0], normed_one, inverse_one)
    attn_grad = grad_sum_one.astype(BF)
    grad_out_w = mm_tn(merged, attn_grad)
    grad_att_bias = jnp.sum(attn_grad.astype(F32), axis=0)
    ctx_grad = heads(mm_nt(attn_grad, w_out).astype(BF))
    local_grad = (ctx_grad.astype(F32) * keep_local[:, None, None]).astype(BF)
    glob_ctx_grad = jnp.einsum(
        "gl,lhe->ghe", select_low, ctx_grad, preferred_element_type=F32
    ).astype(BF)
    key_grad = jnp.zeros(k.shape, F32)
    value_grad = jnp.zeros(v.shape, F32)
    query_parts = []
    for index, offset in enumerate(offsets):
        qb, masked = block_scores(offset)
        probs = jnp.exp(masked - kept[index][0]) / kept[index][1]
        low = probs.astype(BF)
        gb = local_grad[offset : offset + block]
        grad_probs = jnp.einsum("ihe,jhe->hij", gb, v, preferred_element_type=F32)
        dot = jnp.sum(probs * grad_probs, axis=-1, keepdims=True)
        score_grad = (probs * (grad_probs - dot)).astype(BF)
        query_parts.append(jnp.einsum("hij,jhe->ihe", score_grad, k, preferred_element_type=F32))
        key_grad = key_grad + jnp.einsum("hij,ihe->jhe", score_grad, qb, preferred_element_type=F32)
        value_grad = value_grad + jnp.einsum("hij,ihe->jhe", low, gb, preferred_element_type=F32)
    dq = jnp.concatenate(query_parts, axis=0).astype(BF)
    glob_grad_probs = jnp.einsum("ghe,jhe->hgj", glob_ctx_grad, vg, preferred_element_type=F32)
    glob_dot = jnp.sum(glob_probs * glob_grad_probs, axis=-1, keepdims=True)
    glob_score_grad = (glob_probs * (glob_grad_probs - glob_dot)).astype(BF)
    dqg = jnp.einsum("hgj,jhe->ghe", glob_score_grad, kg, preferred_element_type=F32).astype(BF)
    dkg = jnp.einsum("hgj,ghe->jhe", glob_score_grad, qg, preferred_element_type=F32).astype(BF)
    dvg = jnp.einsum("hgj,ghe->jhe", glob_low, glob_ctx_grad, preferred_element_type=F32).astype(BF)

    def flat(value):
        return value.astype(BF).reshape(value.shape[0], width)

    dq, dk, dv, dkg, dvg = (flat(value) for value in (dq, key_grad, value_grad, dkg, dvg))
    pre_query = dq * scale
    glob_pre = flat(dqg) * scale
    token_grad = (
        grad_sum_one
        + mm_nt(pre_query, w_local[0])
        + mm_nt(dk, w_local[1])
        + mm_nt(dv, w_local[2])
        + mm_nt(dkg, w_global[1])
        + mm_nt(dvg, w_global[2])
    )
    token_grad = token_grad + jnp.einsum(
        "gr,gd->rd", select_full, mm_nt(glob_pre, w_global[0]), precision=HIGHEST
    )
    grad_local = jnp.stack([mm_tn(x, pre_query), mm_tn(x, dk), mm_tn(x, dv)])
    grad_global = jnp.stack([mm_tn(rows_glob, glob_pre), mm_tn(x, dkg), mm_tn(x, dvg)])

    def total_of(value):
        return jnp.sum(value.astype(F32), axis=0)

    grad_bias = jnp.stack(
        [
            total_of(pre_query),
            total_of(dv),
            total_of(glob_pre),
            total_of(dvg),
            grad_att_bias,
            grad_out_bias,
        ]
    )
    grad_gain = jnp.stack([grad_gain_one, grad_gain_two])
    grad_shift = jnp.stack([grad_shift_one, grad_shift_two])
    return (
        result.astype(BF),
        token_grad.astype(BF),
        (
            grad_local,
            grad_global,
            grad_out_w,
            grad_bias,
            grad_gain,
            grad_shift,
            grad_in_w,
            grad_in_bias,
            grad_back_w,
        ),
    )


def per_device(
    inputs,
    global_pos,
    w_local,
    w_global,
    w_out,
    b_proj,
    gains,
    shifts,
    w_in,
    c_in,
    w_back,
    cotangent,
):
    sp_count = lax.axis_size("sp")
    fsdp_count = lax.axis_size("fsdp")
    sp_index = lax.axis_index("sp")
    own_seqs = inputs.shape[0] // sp_count
    shard = w_out.shape[0]
    width = w_out.shape[1]
    ff_shard = w_back.shape[0]
    pieces = w_in.shape[1] // width

    def to_sequence(value):
        return lax.all_to_all(value, "sp", split_axis=0, concat_axis=1, tiled=True)

    def to_tokens(value):
        return lax.all_to_all(value, "sp", split_axis=1, concat_axis=0, tiled=True)

    x_all = to_sequence(inputs)
    up_all = to_sequence(cotangent)
    own_pos = lax.dynamic_slice_in_dim(global_pos, sp_index * own_seqs, own_seqs, 0)
    small = jnp.concatenate(
        [b_proj.reshape(-1), gains.reshape(-1), shifts.reshape(-1), c_in.reshape(-1)]
    )
    small_rows = -(-small.shape[0] // width)
    small = jnp.pad(small, (0, small_rows * width - small.shape[0])).reshape(small_rows, width)
    pack_one = jnp.concatenate(
        [w_local.reshape(-1, width), w_global.reshape(-1, width), w_out, small], axis=0
    )
    pack_two = jnp.concatenate(
        [w_in.reshape(shard, pieces, width).transpose(1, 0, 2).reshape(-1, width), w_back], axis=0
    )
    all_one = lax.all_gather(pack_one, "fsdp")
    all_two = lax.all_gather(pack_two, "fsdp")

    def part(packed, start):
        return packed[:, start : start + shard].reshape(fsdp_count * shard, width)

    full_local = [part(all_one, index * shard) for index in range(3)]
    full_global = [part(all_one, (3 + index) * shard) for index in range(3)]
    full_out = part(all_one, 6 * shard)
    small_all = all_one[:, 7 * shard :].reshape(fsdp_count, -1)

    def vectors(start, count):
        taken = small_all[:, start : start + count * shard].reshape(fsdp_count, count, shard)
        return taken.transpose(1, 0, 2).reshape(count, fsdp_count * shard)

    full_bias = vectors(0, 6)
    full_gain = vectors(6 * shard, 2)
    full_shift = vectors(8 * shard, 2)
    full_c = small_all[:, 10 * shard : 10 * shard + ff_shard].reshape(-1)
    full_in = jnp.concatenate([part(all_two, index * shard) for index in range(pieces)], axis=1)
    full_back = all_two[:, pieces * shard :].reshape(-1, width)
    weights = (
        full_local,
        full_global,
        full_out,
        full_bias,
        full_gain,
        full_shift,
        full_in,
        full_c,
        full_back,
    )
    results = []
    token_grads = []
    totals = None
    for index in range(own_seqs):
        result, token_grad, grads = sequence_step(
            x_all[index], own_pos[index], up_all[index], weights
        )
        results.append(result)
        token_grads.append(token_grad)
        totals = grads if totals is None else tuple((a + b for a, b in zip(totals, grads)))
    out = to_tokens(jnp.stack(results))
    grad_inputs = to_tokens(jnp.stack(token_grads))
    g_local, g_global, g_out, g_bias, g_gain, g_shift, g_in, g_c, g_back = totals

    def rows(value):
        return value.astype(BF).reshape(-1, fsdp_count, shard, width).transpose(1, 0, 2, 3)

    def cols(value):
        return value.reshape(-1, fsdp_count, shard).transpose(1, 0, 2).reshape(fsdp_count, -1)

    g_small = jnp.concatenate(
        [cols(g_bias), cols(g_gain), cols(g_shift), g_c.reshape(fsdp_count, ff_shard)], axis=1
    ).astype(BF)
    g_small = jnp.pad(g_small, ((0, 0), (0, small_rows * width - g_small.shape[1])))
    first = jnp.concatenate(
        [
            rows(g_in.reshape(width, pieces, width).transpose(1, 0, 2)).reshape(
                fsdp_count, -1, width
            ),
            g_back.astype(BF).reshape(fsdp_count, ff_shard, width),
        ],
        axis=1,
    )
    second = jnp.concatenate(
        [
            rows(g_local).reshape(fsdp_count, -1, width),
            rows(g_global).reshape(fsdp_count, -1, width),
            rows(g_out).reshape(fsdp_count, -1, width),
            g_small.reshape(fsdp_count, small_rows, width),
        ],
        axis=1,
    )

    def reduce(value):
        mine = lax.psum_scatter(value, "fsdp", scatter_dimension=0, tiled=False)
        return lax.psum(mine, "sp").astype(F32)

    first = reduce(first)
    second = reduce(second)
    small_sum = second[7 * shard :].reshape(-1)
    return (
        out,
        grad_inputs,
        second[: 3 * shard].reshape(3, shard, width),
        second[3 * shard : 6 * shard].reshape(3, shard, width),
        second[6 * shard : 7 * shard],
        small_sum[: 6 * shard].reshape(6, shard),
        small_sum[6 * shard : 8 * shard].reshape(2, shard),
        small_sum[8 * shard : 10 * shard].reshape(2, shard),
        first[: pieces * shard]
        .reshape(pieces, shard, width)
        .transpose(1, 0, 2)
        .reshape(shard, pieces * width),
        small_sum[10 * shard : 10 * shard + ff_shard],
        first[pieces * shard :],
    )


def solution(mesh):
    rows = P("fsdp", None)
    tokens = P("fsdp", "sp", None)
    columns = P(None, "fsdp")
    stacked = P(None, "fsdp", None)
    return jax.shard_map(
        per_device,
        mesh=mesh,
        in_specs=(
            tokens,
            rows,
            stacked,
            stacked,
            rows,
            columns,
            columns,
            columns,
            rows,
            P("fsdp"),
            rows,
            tokens,
        ),
        out_specs=(
            tokens,
            tokens,
            stacked,
            stacked,
            rows,
            columns,
            columns,
            columns,
            rows,
            P("fsdp"),
            rows,
        ),
        check_vma=False,
    )
```

profile of v0, /device:TPU:0, one launch (start us, length us, event | category | flops | bytes accessed | tf_op | source)
XLA Modules:
  0.0 702.7 jit_solution(2198869074152670844)
XLA Ops:
  12.7 43.1 %all_to_all.42 = bf16[4,256,768]{2,1,0:T(8,128)(2,1)S(1)} all-to-all(bf16[4,256,768]{2,1,0:T(8,128)(2,1)S(1)} %copy-done.35), channel_id=1, replica_groups=mesh['fsdp'=8,'sp'=4] {'sp'}, dimensions={0} | all-to-all | bytes 3145728 | tf_op jit(solution)/shard_map/all_to_all | solution.py:231
  67.4 28.0 %all-to-all-done.2 = bf16[4,256,768]{2,1,0:T(8,128)(2,1)S(1)} async-done(((bf16[4,256,768]{2,1,0:T(8,128)(2,1)}), bf16[4,256,768]{2,1,0:T(8,128)(2,1)S(1)}, u32[]{:S(2)}, u32[]{:S(2)}) %all-to-all-start.2) | async-done | bytes 1572896 | tf_op jit(solution)/shard_map/all_to_all | solution.py:231
  135.9 11.0 %fusion.132 = (f32[12,256]{1,0:T(8,128)}, f32[12,256,1024]{2,1,0:T(8,128)}) fusion(pred[256,1024]{1,0:T(8,128)(4,1)} %get-tuple-element.82, bf16[256,12,64]{0,2,1:T(8,128)(2,1)} %bitcast.334, bf16[1024,12,64]{0,2,1:T(8,128)(2,1)} %bitcast.255), kind=kOutput, calls=%fused_computation.236 | convolution fusion | flops 412091392 | bytes 14823424 | tf_op jit(solution)/shard_map/sub | solution.py:88
  146.9 10.7 %fusion.133 = (f32[12,256]{1,0:T(8,128)}, f32[12,256,1024]{2,1,0:T(8,128)}) fusion(pred[256,1024]{1,0:T(8,128)(4,1)} %get-tuple-element.81, bf16[256,12,64]{0,2,1:T(8,128)(2,1)} %bitcast.311, bf16[1024,12,64]{0,2,1:T(8,128)(2,1)} %bitcast.256), kind=kOutput, calls=%fused_computation.237 | convolution fusion | flops 412091392 | bytes 14823424 | tf_op jit(solution)/shard_map/sub | solution.py:88
  157.6 10.8 %fusion.134 = (f32[12,256]{1,0:T(8,128)}, f32[12,256,1024]{2,1,0:T(8,128)}) fusion(pred[256,1024]{1,0:T(8,128)(4,1)} %get-tuple-element.80, bf16[256,12,64]{0,2,1:T(8,128)(2,1)} %bitcast.309, bf16[1024,12,64]{0,2,1:T(8,128)(2,1)} %bitcast.257), kind=kOutput, calls=%fused_computation.238 | convolution fusion | flops 412091392 | bytes 14823424 | tf_op jit(solution)/shard_map/sub | solution.py:88
  168.5 11.1 %fusion.135 = (f32[12,256]{1,0:T(8,128)}, f32[12,256,1024]{2,1,0:T(8,128)}) fusion(pred[256,1024]{1,0:T(8,128)(4,1)} %get-tuple-element.79, bf16[256,12,64]{0,2,1:T(8,128)(2,1)S(1)} %bitcast.307, bf16[1024,12,64]{0,2,1:T(8,128)(2,1)} %bitcast.258), kind=kOutput, calls=%fused_computation.239 | convolution fusion | flops 412091392 | bytes 14823424 | tf_op jit(solution)/shard_map/sub | solution.py:88
  217.1 14.2 %multiply_convert_fusion.4 = (bf16[1024,3072]{1,0:T(8,128)(2,1)}, f32[1024,3072]{1,0:T(8,128)}) fusion(f32[3072]{0:T(1024)S(1)} %copy-done.85, bf16[768,768]{1,0:T(8,128)(2,1)} %bitcast.351, bf16[768,768]{1,0:T(8,128)(2,1)} %bitcast.353, bf16[768,768]{1,0:T(8,128)(2,1)} %bitcast.355, bf16[768,768]{1,0:T(8,128)(2,1)} %bitcast.349, ...), kind=kOutput, calls=%fused_computation.20 | convolution fusion | flops 4873519104 | bytes 26765312 | tf_op jit(solution)/shard_map/dot_general | solution.py:31
  231.4 7.7 %fusion.138 = (f32[1024]{0:T(1024)S(1)}, f32[1024,768]{0,1:T(8,128)S(1)}) fusion(f32[768]{0:T(1024)S(1)} %copy-done.96, bf16[1024,3072]{1,0:T(8,128)(2,1)} %get-tuple-element.95, bf16[3072,768]{1,0:T(8,128)(2,1)S(1)} %bitcast.303, f32[768]{0:T(1024)S(1)} %copy-done.94, f32[768]{0:T(1024)S(1)} %mul.222, f32[1024]{0:T(1024)S(1)} %add_rsqrt_fusion.1, ...), kind=kOutput, calls=%fused_computation.242 | convolution fusion | flops 4837342208 | bytes 17323008 | tf_op jit(solution)/shard_map/dot_general | solution.py:31
  244.4 15.1 %fusion.140 = (bf16[3072]{0:T(1024)(128)(2,1)}, bf16[1024,3072]{1,0:T(8,128)(2,1)}) fusion(f32[1024,3072]{1,0:T(8,128)} %get-tuple-element.96, f32[3072]{0:T(1024)S(1)} %copy-done.85, bf16[3072,768]{1,0:T(8,128)(2,1)S(1)} %bitcast.304, f32[1024,768]{0,1:T(8,128)S(1)} %get-tuple-element.52), kind=kOutput, calls=%fused_computation.244 | convolution fusion | flops 4870370304 | bytes 26757120 | tf_op jit(solution)/shard_map/dot_general | solution.py:35
  259.6 9.4 %multiply_reduce_fusion.5 = (bf16[768]{0:T(1024)(128)(2,1)}, f32[1024]{0:T(1024)S(1)}, f32[1024]{0:T(1024)S(1)}, bf16[768]{0:T(1024)(128)(2,1)}, f32[1024,768]{0,1:T(8,128)S(1)}) fusion(f32[1024,768]{0,1:T(8,128)S(1)} %copy-done.14, f32[1024]{0:T(1024)S(1)} %add_rsqrt_fusion.1, f32[1024]{0:T(1024)S(1)} %broadcast_multiply_fusion.4, f32[768]{0:T(1024)S(1)} %mul.222, ...), kind=kOutput, calls=%fused_computation.57 | convolution fusion | flops 4858572800 | bytes 20469760 | tf_op jit(solution)/shard_map/dot_general | solution.py:35
  282.7 8.0 %fusion.41 = f32[12,64,1024]{2,1,0:T(8,128)} fusion(bf16[1024,12,64]{0,2,1:T(8,128)(2,1)S(1)} %multiply_convert_fusion.5, f32[12,256,1024]{2,1,0:T(8,128)} %get-tuple-element.88, f32[12,256]{1,0:T(8,128)S(1)} %copy-done.80), kind=kOutput, calls=%fused_computation.82 | convolution fusion | flops 408944640 | bytes 16138240 | tf_op jit(solution)/shard_map/hij,ihe->jhe/dot_general | solution.py:146
  290.7 8.4 %fusion.37 = f32[12,64,1024]{2,1,0:T(8,128)} fusion(bf16[1024,12,64]{0,2,1:T(8,128)(2,1)S(1)} %multiply_convert_fusion.5, f32[12,256,1024]{2,1,0:T(8,128)} %get-tuple-element.86, f32[12,256]{1,0:T(8,128)S(1)} %copy-done.82), kind=kOutput, calls=%fused_computation.78 | convolution fusion | flops 408944640 | bytes 16138240 | tf_op jit(solution)/shard_map/hij,ihe->jhe/dot_general | solution.py:146
  302.4 8.2 %multiply_reduce_fusion = (f32[12,256]{1,0:T(8,128)}, f32[12,256,1024]{2,1,0:T(8,128)}) fusion(f32[12,256,1024]{2,1,0:T(8,128)S(1)} %bitcast.286, f32[12,256]{1,0:T(8,128)S(1)} %copy-done.78, bf16[1024,12,64]{0,2,1:T(8,128)(2,1)} %bitcast.382, bf16[1024,12,64]{0,2,1:T(8,128)(2,1)S(1)} %multiply_convert_fusion.5), kind=kOutput, calls=%fused_computation.13 | convolution fusion | flops 412087296 | bytes 27160576 | tf_op jit(solution)/shard_map/ihe,jhe->hij/dot_general | solution.py:141
  329.4 7.4 %multiply_reduce_fusion.2 = (f32[12,256]{1,0:T(8,128)S(1)}, f32[12,256,1024]{2,1,0:T(8,128)}) fusion(f32[12,256,1024]{2,1,0:T(8,128)S(1)} %bitcast.290, f32[12,256]{1,0:T(8,128)S(1)} %copy-done.81, bf16[1024,12,64]{0,2,1:T(8,128)(2,1)} %bitcast.384, bf16[1024,12,64]{0,2,1:T(8,128)(2,1)S(1)} %copy-done.40), kind=kOutput, calls=%fused_computation.17 | convolution fusion | flops 412087296 | bytes 27160576 | tf_op jit(solution)/shard_map/ihe,jhe->hij/dot_general | solution.py:141
  348.8 7.6 %multiply_reduce_fusion.3 = (f32[12,256]{1,0:T(8,128)S(1)}, f32[12,256,1024]{2,1,0:T(8,128)}) fusion(f32[12,256,1024]{2,1,0:T(8,128)S(1)} %bitcast.282, f32[12,256]{1,0:T(8,128)S(1)} %copy-done.76, bf16[1024,12,64]{0,2,1:T(8,128)(2,1)} %bitcast.385, bf16[1024,12,64]{0,2,1:T(8,128)(2,1)S(1)} %copy-done.40), kind=kOutput, calls=%fused_computation.19 | convolution fusion | flops 412087296 | bytes 27160576 | tf_op jit(solution)/shard_map/ihe,jhe->hij/dot_general | solution.py:141
  443.7 10.5 %convolution_convert_fusion.1 = bf16[768,3072]{1,0:T(8,128)(2,1)} fusion(bf16[1024,3072]{1,0:T(8,128)(2,1)} %get-tuple-element.117, f32[1024,768]{0,1:T(8,128)S(1)} %copy-done.15, f32[768]{0:T(1024)S(1)} %copy-done.95, f32[768]{0:T(1024)S(1)} %copy-done.72, f32[1024]{0:T(1024)S(1)} %copy-done.74, f32[1024]{0:T(1024)S(1)} %copy-done.67), kind=kOutput, calls=%fused_computation.49 | convolution fusion | flops 4838129664 | bytes 14170112 | tf_op jit(solution)/shard_map/dot_general | solution.py:39
  454.2 9.9 %convert_element_type.322 = bf16[768,4,768]{2,1,0:T(4,128)(2,1)} reshape(bf16[768,3072]{1,0:T(8,128)(2,1)} %convolution_convert_fusion.1) | data formatting | bytes 9437184 | tf_op jit(solution)/shard_map/convert_element_type | solution.py:297
  468.1 8.6 %convolution_convert_fusion = bf16[3072,768]{1,0:T(8,128)(2,1)S(1)} fusion(bf16[1024,3072]{1,0:T(8,128)(2,1)} %get-tuple-element.95, f32[1024,768]{0,1:T(8,128)S(1)} %copy-done.22), kind=kOutput, calls=%fused_computation.48 | convolution fusion | flops 4834983936 | bytes 14155776 | tf_op jit(solution)/shard_map/dot_general | solution.py:39
  481.5 7.6 %copy.94 = bf16[1,1024,768]{2,0,1:T(2,128)(2,1)S(1)} copy(bf16[1,1024,768]{1,2,0:T(8,128)(2,1)} %get-tuple-element.66) | data formatting | bytes 3145728 | tf_op jit(solution)/shard_map/stack | solution.py:292
  489.7 11.8 %reduce.65 = bf16[1024,768]{1,0:T(8,128)(2,1)} reduce(bf16[1024,1,768]{2,1,0:T(2,128)(2,1)S(1)} %bitcast.293, bf16[]{:T(256)} %broadcast.289), dimensions={1}, to_apply=%bitcast.153.reduce_sub_computation | reduce | bytes 3145730
  522.8 7.6 %copy.105 = bf16[1,1024,768]{2,0,1:T(2,128)(2,1)S(1)} copy(bf16[1,1024,768]{1,2,0:T(8,128)(2,1)} %fusion.51) | data formatting | bytes 3145728 | tf_op jit(solution)/shard_map/stack | solution.py:293
  530.4 11.8 %reduce.66 = bf16[1024,768]{1,0:T(8,128)(2,1)} reduce(bf16[1024,1,768]{2,1,0:T(2,128)(2,1)S(1)} %bitcast.294, bf16[]{:T(256)} %broadcast.289), dimensions={1}, to_apply=%bitcast.155.reduce_sub_computation | reduce | bytes 3145730
  551.1 41.6 %reduce-scatter.5.cloned.1.call-done = bf16[1,768,768]{2,1,0:T(8,128)(2,1)} async-done(((bf16[8,768,768]{2,1,0:T(8,128)(2,1)}), bf16[1,768,768]{2,1,0:T(8,128)(2,1)}) %reduce-scatter.5.cloned.1.call-update) | async-done | bytes 1179664 | tf_op jit(solution)/shard_map/reduce_scatter | solution.py:326
  601.7 85.1 %all-reduce.5.cloned.1.call-done = (bf16[674,768]{1,0:T(8,128)(2,1)}, bf16[768,768]{1,0:T(8,128)(2,1)}) async-done(((bf16[674,768]{1,0:T(8,128)(2,1)}, bf16[768,768]{1,0:T(8,128)(2,1)}), (bf16[674,768]{1,0:T(8,128)(2,1)}, bf16[768,768]{1,0:T(8,128)(2,1)})) %all-reduce.5.cloned.1.call-update) | async-done | bytes 2214928 | tf_op jit(solution)/shard_map/psum | solution.py:327
  (450 shorter events, 291.9 us)
Async XLA Ops:
  7.2 55.6 %copy-start = (s32[4,4]{1,0:T(4,128)S(1)}, s32[4,4]{1,0:T(4,128)}, u32[]{:S(2)}) copy-start(s32[4,4]{1,0:T(4,128)} %param.13) | copy-start | bytes 196
  7.2 91.1 %all-gather.8.cloned.1.call-start = ((), (), s32[]{:S(2)}) async-start(), calls=%async_computation.9 | async-start | bytes 9400320 | tf_op jit(solution)/shard_map/all_gather | solution.py:250
  55.8 39.7 %all-to-all-start.2 = ((bf16[4,256,768]{2,1,0:T(8,128)(2,1)}), bf16[4,256,768]{2,1,0:T(8,128)(2,1)S(1)}, u32[]{:S(2)}, u32[]{:S(2)}) async-start(bf16[4,256,768]{2,1,0:T(8,128)(2,1)} %param.23), calls=%async_computation.2 | async-start | bytes 3145728 | tf_op jit(solution)/shard_map/all_to_all | solution.py:231
  59.4 147.3 %all-gather.6.cloned.1.call-start = ((), (), s32[]{:S(2)}) async-start(), calls=%async_computation.8 | async-start | bytes 10616832 | tf_op jit(solution)/shard_map/all_gather | solution.py:251
  62.7 488.4 %reduce-scatter.3.cloned.1.call-start = ((), (), s32[]{:S(2)}) async-start(), calls=%async_computation.6 | async-start | bytes 9400320 | tf_op jit(solution)/shard_map/reduce_scatter | solution.py:326
  62.8 33.0 %copy-start.86 = (s32[4]{0:T(128)}, s32[4]{0:T(128)S(1)}, u32[]{:S(2)}) copy-start(s32[4]{0:T(128)S(1)} %dynamic-slice_bitcast_fusion) | copy-start | bytes 52
  101.0 168.0 %copy-start.71 = (f32[768]{0:T(1024)}, f32[768]{0:T(1024)S(1)}, u32[]{:S(2)}) copy-start(f32[768]{0:T(1024)S(1)} %mul.222) | copy-start | bytes 9220
  129.3 39.1 %copy-start.23 = (bf16[256,768]{0,1:T(8,128)(2,1)}, bf16[256,768]{0,1:T(8,128)(2,1)S(1)}, u32[]{:S(2)}) copy-start(bf16[256,768]{0,1:T(8,128)(2,1)S(1)} %get-tuple-element.67) | copy-start | bytes 1179652
  204.5 64.4 %copy-start.66 = (f32[1024]{0:T(1024)}, f32[1024]{0:T(1024)S(1)}, u32[]{:S(2)}) copy-start(f32[1024]{0:T(1024)S(1)} %broadcast_multiply_fusion.4) | copy-start | bytes 12292
  206.7 62.3 %copy-start.73 = (f32[1024]{0:T(1024)}, f32[1024]{0:T(1024)S(1)}, u32[]{:S(2)}) copy-start(f32[1024]{0:T(1024)S(1)} %add_rsqrt_fusion.1) | copy-start | bytes 12292
  217.1 14.3 %copy-start.96 = (f32[768]{0:T(1024)S(1)}, f32[768]{0:T(1024)}, u32[]{:S(2)}) copy-start(f32[768]{0:T(1024)} %add.238) | copy-start | bytes 9220
  244.4 15.1 %copy-start.21 = (f32[1024,768]{0,1:T(8,128)}, f32[1024,768]{0,1:T(8,128)S(1)}, u32[]{:S(2)}) copy-start(f32[1024,768]{0,1:T(8,128)S(1)} %get-tuple-element.52) | copy-start | bytes 9437188
  244.4 15.1 %copy-start.53 = (bf16[8,96,768]{2,1,0:T(8,128)(2,1)S(1)}, bf16[8,96,768]{2,1,0:T(8,128)(2,1)}, u32[]{:S(2)}) copy-start(bf16[8,96,768]{2,1,0:T(8,128)(2,1)} %get-tuple-element.55) | copy-start | bytes 3538948
  244.4 15.1 %copy-start.54 = (bf16[8,96,768]{2,1,0:T(8,128)(2,1)S(1)}, bf16[8,96,768]{2,1,0:T(8,128)(2,1)}, u32[]{:S(2)}) copy-start(bf16[8,96,768]{2,1,0:T(8,128)(2,1)} %get-tuple-element.56) | copy-start | bytes 3538948
  244.4 15.1 %copy-start.55 = (bf16[8,96,768]{2,1,0:T(8,128)(2,1)S(1)}, bf16[8,96,768]{2,1,0:T(8,128)(2,1)}, u32[]{:S(2)}) copy-start(bf16[8,96,768]{2,1,0:T(8,128)(2,1)} %get-tuple-element.57) | copy-start | bytes 3538948
  244.4 15.1 %copy-start.56 = (bf16[8,96,768]{2,1,0:T(8,128)(2,1)S(1)}, bf16[8,96,768]{2,1,0:T(8,128)(2,1)}, u32[]{:S(2)}) copy-start(bf16[8,96,768]{2,1,0:T(8,128)(2,1)} %get-tuple-element.58) | copy-start | bytes 3538948
  275.8 34.8 %copy-start.39 = (bf16[1024,12,64]{0,2,1:T(8,128)(2,1)}, bf16[1024,12,64]{0,2,1:T(8,128)(2,1)S(1)}, u32[]{:S(2)}) copy-start(bf16[1024,12,64]{0,2,1:T(8,128)(2,1)S(1)} %multiply_convert_fusion.5) | copy-start | bytes 4718596
  282.7 16.4 %slice-start.9 = ((s8[12582912]{0:T(1024)(128)(4,1)}), s8[4194304]{0:T(1024)(128)(4,1)S(1)}, s32[]{:S(2)}) async-start(s8[12582912]{0:T(1024)(128)(4,1)} %bitcast.285), calls=%async_computation.20 | async-start | bytes 8388608
  282.7 16.4 %slice-start.10 = ((s8[12582912]{0:T(1024)(128)(4,1)}), s8[4194304]{0:T(1024)(128)(4,1)S(1)}, s32[]{:S(2)}) async-start(s8[12582912]{0:T(1024)(128)(4,1)} %bitcast.285), calls=%async_computation.21 | async-start | bytes 8388608
  344.8 33.2 %copy-start.27 = (bf16[12,64,256]{2,1,0:T(8,128)(2,1)}, bf16[12,64,256]{2,1,0:T(8,128)(2,1)S(1)}, u32[]{:S(2)}) copy-start(bf16[12,64,256]{2,1,0:T(8,128)(2,1)S(1)} %convolution_convert_fusion.16) | copy-start | bytes 1179652
  441.9 150.9 %reduce-scatter.5.cloned.1.call-start = ((), (), s32[]{:S(2)}) async-start(), calls=%async_computation.7 | async-start | bytes 10616832 | tf_op jit(solution)/shard_map/reduce_scatter | solution.py:326
  505.3 40.7 %all-to-all-start.1 = ((bf16[4,2,98304]{2,1,0:T(2,128)(2,1)}), bf16[4,2,98304]{2,1,0:T(2,128)(2,1)}, u32[]{:S(2)}, u32[]{:S(2)}) async-start(bf16[4,2,98304]{2,1,0:T(2,128)(2,1)} %reshape.661), calls=%async_computation.1 | async-start | bytes 3145728 | tf_op jit(solution)/shard_map/all_to_all | solution.py:234
  546.0 51.2 %all-to-all-start.3 = ((bf16[4,2,98304]{2,1,0:T(2,128)(2,1)}), bf16[4,2,98304]{2,1,0:T(2,128)(2,1)}, u32[]{:S(2)}, u32[]{:S(2)}) async-start(bf16[4,2,98304]{2,1,0:T(2,128)(2,1)} %reshape.663), calls=%async_computation.3 | async-start | bytes 3145728 | tf_op jit(solution)/shard_map/all_to_all | solution.py:234
  551.1 135.7 %all-reduce.5.cloned.1.call-start = ((), (), s32[]{:S(2)}) async-start(), calls=%async_computation.10 | async-start | bytes 4448256 | tf_op jit(solution)/shard_map/psum | solution.py:327
  (112 other events, 473.0 us)
Sparse Core Ops, SparseCore 0:
  12.8 56.9 all-gather.7
  72.3 58.8 all-gather.5
  442.0 70.4 reduce-scatter.2
  516.2 76.4 reduce-scatter.4
  595.2 91.5 all-reduce.4
where the time goes:
time: 709 us; the launch traced here: 703 us
  matrix products  269 us (38%)
  waiting for transfers between devices  155 us (22%)
  local copies, waits for them, and re-layouts  129 us (18%)
  other arithmetic  77.2 us (11%)
  blocking collectives  43.1 us (6%)
  between operations  15.4 us (2%)
  starting transfers between devices  13.4 us (2%)
    psum x1, waiting for transfers between devices, reduce(): return lax.psum(mine, 'sp').astype(F32)  85.1 us
    sub x4, matrix products, sequence_step(): powers = jnp.exp(masked - top)  43.7 us
    all_to_all x1, blocking collectives, to_sequence(): return lax.all_to_all(value, 'sp', split_axis=0, concat_axis=1, tiled=True)  43.1 us
    unnamed x271, local copies, waits for them, and re-layouts  42.3 us
    reduce_scatter x2, waiting for transfers between devices, reduce(): mine = lax.psum_scatter(value, 'fsdp', scatter_dimension=0, tiled=False)  41.6 us
    dot_general x9, matrix products, mm_tn(): lax.dot_general(a, b, (((0,), (0,)), ((), ())), preferred_element_type=F32)  38.9 us
    dot_general x10, matrix products, mm(): return jnp.dot(a, b, preferred_element_type=F32)  38.8 us
    dot_general x9, matrix products, mm_nt(): lax.dot_general(a, b, (((1,), (1,)), ((), ())), preferred_element_type=F32)  33.3 us
  transfers between devices with their start and end apart: 8, of which 3 were waited for; matrix products, arithmetic and copies ran while one was open for 31% of the time, Pallas kernels for 0%

commit v1 on v0

--- a/solution.py
+++ b/solution.py
@@ -11,6 +11,12 @@
 NORM_EPS = 1e-05
 BF = jnp.bfloat16
 F32 = jnp.float32
+
+
+def add_all(shard, axis):
+    parts = lax.all_gather(shard, axis, axis=0, tiled=False)
+    total = parts.sum(axis=0)
+    return total
 
 
 def normalize(summed):
@@ -324,7 +330,7 @@
 
     def reduce(value):
         mine = lax.psum_scatter(value, "fsdp", scatter_dimension=0, tiled=False)
-        return lax.psum(mine, "sp").astype(F32)
+        return add_all(mine, "sp").astype(F32)
 
     first = reduce(first)
     second = reduce(second)

time: 709 us -> 838 us (1.18)
  waiting for transfers between devices: 155 us -> 280 us
    all_to_all x2, waiting for transfers between devices: 0.01 us -> 112 us  [to_tokens(): return lax.all_to_all(value, 'sp', split_axis=1, concat_axis=0, tiled=True)]
    psum x1 -> x0, waiting for transfers between devices: 85.1 us -> none  [reduce(): return lax.psum(mine, 'sp').astype(F32)]
    reduce_scatter x2, waiting for transfers between devices: 41.6 us -> 112 us  [reduce(): mine = lax.psum_scatter(value, 'fsdp', scatter_dimension=0, tiled=False)]
    all_gather x0 -> x2, waiting for transfers between devices: none -> 28.6 us  [add_all(): parts = lax.all_gather(shard, axis, axis=0, tiled=False)]
    unnamed x271 -> x269, local copies, waits for them, and re-layouts: 42.3 us -> 41.3 us
  transfers between devices with their start and end apart: 8 -> 9, of which waited for: 3 -> 6; matrix products, arithmetic and copies ran while one was open for 31% -> 27% of each run, Pallas kernels for 0% -> 0%
where the time goes in v1:
time: 838 us; the launch traced here: 832 us
  waiting for transfers between devices  280 us (33%)
  matrix products  269 us (32%)
  local copies, waits for them, and re-layouts  125 us (15%)
  other arithmetic  84.6 us (10%)
  blocking collectives  43.1 us (5%)
  between operations  16 us (2%)
  starting transfers between devices  13.3 us (2%)
    all_to_all x2, waiting for transfers between devices, to_tokens(): return lax.all_to_all(value, 'sp', split_axis=1, concat_axis=0, tiled=True)  112 us
    reduce_scatter x2, waiting for transfers between devices, reduce(): mine = lax.psum_scatter(value, 'fsdp', scatter_dimension=0, tiled=False)  112 us
    sub x4, matrix products, sequence_step(): powers = jnp.exp(masked - top)  43.6 us
    all_to_all x1, blocking collectives, to_sequence(): return lax.all_to_all(value, 'sp', split_axis=0, concat_axis=1, tiled=True)  43.1 us
    unnamed x269, local copies, waits for them, and re-layouts  41.3 us
    dot_general x9, matrix products, mm_tn(): lax.dot_general(a, b, (((0,), (0,)), ((), ())), preferred_element_type=F32)  38.9 us
    dot_general x10, matrix products, mm(): return jnp.dot(a, b, preferred_element_type=F32)  38.9 us
    dot_general x9, matrix products, mm_nt(): lax.dot_general(a, b, (((1,), (1,)), ((), ())), preferred_element_type=F32)  33.5 us
  transfers between devices with their start and end apart: 9, of which 6 were waited for; matrix products, arithmetic and copies ran while one was open for 27% of the time, Pallas kernels for 0%

profile of v1, /device:TPU:0, one launch (start us, length us, event | category | flops | bytes accessed | tf_op | source)
XLA Modules:
  0.0 831.6 jit_solution(6843104572083162282)
XLA Ops:
  12.7 43.1 %all_to_all.42 = bf16[4,256,768]{2,1,0:T(8,128)(2,1)S(1)} all-to-all(bf16[4,256,768]{2,1,0:T(8,128)(2,1)S(1)} %copy-done.34), channel_id=1, replica_groups=mesh['fsdp'=8,'sp'=4] {'sp'}, dimensions={0} | all-to-all | bytes 3145728 | tf_op jit(solution)/shard_map/all_to_all | solution.py:237
  67.4 28.0 %all-to-all-done.2 = bf16[4,256,768]{2,1,0:T(8,128)(2,1)S(1)} async-done(((bf16[4,256,768]{2,1,0:T(8,128)(2,1)}), bf16[4,256,768]{2,1,0:T(8,128)(2,1)S(1)}, u32[]{:S(2)}, u32[]{:S(2)}) %all-to-all-start.2) | async-done | bytes 1572896 | tf_op jit(solution)/shard_map/all_to_all | solution.py:237
  135.9 11.2 %fusion.132 = (f32[12,256]{1,0:T(8,128)}, f32[12,256,1024]{2,1,0:T(8,128)}) fusion(pred[256,1024]{1,0:T(8,128)(4,1)} %get-tuple-element.80, bf16[256,12,64]{0,2,1:T(8,128)(2,1)} %bitcast.338, bf16[1024,12,64]{0,2,1:T(8,128)(2,1)} %bitcast.259), kind=kOutput, calls=%fused_computation.236 | convolution fusion | flops 412091392 | bytes 14823424 | tf_op jit(solution)/shard_map/sub | solution.py:94
  147.1 10.7 %fusion.133 = (f32[12,256]{1,0:T(8,128)}, f32[12,256,1024]{2,1,0:T(8,128)}) fusion(pred[256,1024]{1,0:T(8,128)(4,1)} %get-tuple-element.79, bf16[256,12,64]{0,2,1:T(8,128)(2,1)} %bitcast.315, bf16[1024,12,64]{0,2,1:T(8,128)(2,1)} %bitcast.260), kind=kOutput, calls=%fused_computation.237 | convolution fusion | flops 412091392 | bytes 14823424 | tf_op jit(solution)/shard_map/sub | solution.py:94
  157.8 10.8 %fusion.134 = (f32[12,256]{1,0:T(8,128)}, f32[12,256,1024]{2,1,0:T(8,128)}) fusion(pred[256,1024]{1,0:T(8,128)(4,1)} %get-tuple-element.78, bf16[256,12,64]{0,2,1:T(8,128)(2,1)} %bitcast.313, bf16[1024,12,64]{0,2,1:T(8,128)(2,1)} %bitcast.261), kind=kOutput, calls=%fused_computation.238 | convolution fusion | flops 412091392 | bytes 14823424 | tf_op jit(solution)/shard_map/sub | solution.py:94
  168.7 10.8 %fusion.135 = (f32[12,256]{1,0:T(8,128)}, f32[12,256,1024]{2,1,0:T(8,128)}) fusion(pred[256,1024]{1,0:T(8,128)(4,1)} %get-tuple-element.77, bf16[256,12,64]{0,2,1:T(8,128)(2,1)S(1)} %bitcast.311, bf16[1024,12,64]{0,2,1:T(8,128)(2,1)} %bitcast.262), kind=kOutput, calls=%fused_computation.239 | convolution fusion | flops 412091392 | bytes 14823424 | tf_op jit(solution)/shard_map/sub | solution.py:94
  217.1 14.3 %multiply_convert_fusion.4 = (bf16[1024,3072]{1,0:T(8,128)(2,1)}, f32[1024,3072]{1,0:T(8,128)}) fusion(f32[3072]{0:T(1024)S(1)} %copy-done.84, bf16[768,768]{1,0:T(8,128)(2,1)} %bitcast.355, bf16[768,768]{1,0:T(8,128)(2,1)} %bitcast.357, bf16[768,768]{1,0:T(8,128)(2,1)} %bitcast.359, bf16[768,768]{1,0:T(8,128)(2,1)} %bitcast.353, ...), kind=kOutput, calls=%fused_computation.20 | convolution fusion | flops 4873519104 | bytes 26765312 | tf_op jit(solution)/shard_map/dot_general | solution.py:37
  231.4 7.7 fusion.138
  244.4 15.3 %fusion.140 = (bf16[3072]{0:T(1024)(128)(2,1)}, bf16[1024,3072]{1,0:T(8,128)(2,1)}) fusion(f32[1024,3072]{1,0:T(8,128)} %get-tuple-element.94, f32[3072]{0:T(1024)S(1)} %copy-done.84, bf16[3072,768]{1,0:T(8,128)(2,1)S(1)} %bitcast.308, f32[1024,768]{0,1:T(8,128)S(1)} %get-tuple-element.50), kind=kOutput, calls=%fused_computation.244 | convolution fusion | flops 4870370304 | bytes 26757120 | tf_op jit(solution)/shard_map/dot_general | solution.py:41
  259.8 9.4 %multiply_reduce_fusion.5 = (bf16[768]{0:T(1024)(128)(2,1)}, f32[1024]{0:T(1024)S(1)}, f32[1024]{0:T(1024)S(1)}, bf16[768]{0:T(1024)(128)(2,1)}, f32[1024,768]{0,1:T(8,128)S(1)}) fusion(f32[1024,768]{0,1:T(8,128)S(1)} %copy-done.14, f32[1024]{0:T(1024)S(1)} %add_rsqrt_fusion.1, f32[1024]{0:T(1024)S(1)} %broadcast_multiply_fusion.4, f32[768]{0:T(1024)S(1)} %mul.222, ...), kind=kOutput, calls=%fused_computation.57 | convolution fusion | flops 4858572800 | bytes 20469760 | tf_op jit(solution)/shard_map/dot_general | solution.py:41
  282.9 8.0 fusion.41
  290.9 8.2 fusion.37
  302.3 8.2 multiply_reduce_fusion
  348.8 7.7 multiply_reduce_fusion.3
  443.4 10.5 %convolution_convert_fusion.1 = bf16[768,3072]{1,0:T(8,128)(2,1)} fusion(bf16[1024,3072]{1,0:T(8,128)(2,1)} %get-tuple-element.115, f32[1024,768]{0,1:T(8,128)S(1)} %copy-done.15, f32[768]{0:T(1024)S(1)} %copy-done.94, f32[768]{0:T(1024)S(1)} %copy-done.71, f32[1024]{0:T(1024)S(1)} %copy-done.73, f32[1024]{0:T(1024)S(1)} %copy-done.66), kind=kOutput, calls=%fused_computation.49 | convolution fusion | flops 4838129664 | bytes 14170112 | tf_op jit(solution)/shard_map/dot_general | solution.py:45
  453.9 10.0 %convert_element_type.326 = bf16[768,4,768]{2,1,0:T(4,128)(2,1)} reshape(bf16[768,3072]{1,0:T(8,128)(2,1)} %convolution_convert_fusion.1) | data formatting | bytes 9437184 | tf_op jit(solution)/shard_map/convert_element_type | solution.py:303
  468.0 8.6 %convolution_convert_fusion = bf16[3072,768]{1,0:T(8,128)(2,1)S(1)} fusion(bf16[1024,3072]{1,0:T(8,128)(2,1)} %get-tuple-element.93, f32[1024,768]{0,1:T(8,128)S(1)} %copy-done.21), kind=kOutput, calls=%fused_computation.48 | convolution fusion | flops 4834983936 | bytes 14155776 | tf_op jit(solution)/shard_map/dot_general | solution.py:45
  480.7 31.5 %reduce-scatter.3.cloned.1.call-done = bf16[1,674,768]{2,1,0:T(8,128)(2,1)} async-done(((bf16[8,674,768]{2,1,0:T(8,128)(2,1)}), bf16[1,674,768]{2,1,0:T(8,128)(2,1)}) %reduce-scatter.3.cloned.1.call-update) | async-done | bytes 1035280 | tf_op jit(solution)/shard_map/reduce_scatter | solution.py:332
  512.2 80.2 %reduce-scatter.5.cloned.1.call-done = bf16[1,768,768]{2,1,0:T(8,128)(2,1)} async-done(((bf16[8,768,768]{2,1,0:T(8,128)(2,1)}), bf16[1,768,768]{2,1,0:T(8,128)(2,1)}) %reduce-scatter.5.cloned.1.call-update) | async-done | bytes 1179664 | tf_op jit(solution)/shard_map/reduce_scatter | solution.py:332
  600.4 11.8 %reduce.67 = bf16[1024,768]{1,0:T(8,128)(2,1)} reduce(bf16[1024,1,768]{2,1,0:T(2,128)(2,1)S(1)} %bitcast.297, bf16[]{:T(256)} %broadcast.289), dimensions={1}, to_apply=%bitcast.157.reduce_sub_computation | reduce | bytes 3145730
  641.3 11.8 %reduce.68 = bf16[1024,768]{1,0:T(8,128)(2,1)} reduce(bf16[1024,1,768]{2,1,0:T(2,128)(2,1)S(1)} %bitcast.298, bf16[]{:T(256)} %broadcast.289), dimensions={1}, to_apply=%bitcast.159.reduce_sub_computation | reduce | bytes 3145730
  656.8 42.8 %all-to-all-done.1 = bf16[4,2,98304]{2,1,0:T(2,128)(2,1)} async-done(((bf16[4,2,98304]{2,1,0:T(2,128)(2,1)}), bf16[4,2,98304]{2,1,0:T(2,128)(2,1)}, u32[]{:S(2)}, u32[]{:S(2)}) %all-to-all-start.1) | async-done | bytes 1572896 | tf_op jit(solution)/shard_map/all_to_all | solution.py:240
  708.7 69.0 %all-to-all-done.3 = bf16[4,2,98304]{2,1,0:T(2,128)(2,1)} async-done(((bf16[4,2,98304]{2,1,0:T(2,128)(2,1)}), bf16[4,2,98304]{2,1,0:T(2,128)(2,1)}, u32[]{:S(2)}, u32[]{:S(2)}) %all-to-all-start.3) | async-done | bytes 1572896 | tf_op jit(solution)/shard_map/all_to_all | solution.py:240
  789.6 28.6 %all-gather.10.cloned.1.call-done = bf16[4,768,768]{2,1,0:T(8,128)(2,1)} async-done(((bf16[1,768,768]{2,1,0:T(8,128)(2,1)}), bf16[4,768,768]{2,1,0:T(8,128)(2,1)}) %all-gather.10.cloned.1.call-update) | async-done | bytes 4718608 | tf_op jit(solution)/shard_map/all_gather | solution.py:17
  (452 shorter events, 317.5 us)
Async XLA Ops:
  7.2 55.6 %copy-start = (s32[4,4]{1,0:T(4,128)S(1)}, s32[4,4]{1,0:T(4,128)}, u32[]{:S(2)}) copy-start(s32[4,4]{1,0:T(4,128)} %param.13) | copy-start | bytes 196
  7.2 91.1 %all-gather.14.cloned.1.call-start = ((), (), s32[]{:S(2)}) async-start(), calls=%async_computation.11 | async-start | bytes 9400320 | tf_op jit(solution)/shard_map/all_gather | solution.py:256
  55.8 39.7 %all-to-all-start.2 = ((bf16[4,256,768]{2,1,0:T(8,128)(2,1)}), bf16[4,256,768]{2,1,0:T(8,128)(2,1)S(1)}, u32[]{:S(2)}, u32[]{:S(2)}) async-start(bf16[4,256,768]{2,1,0:T(8,128)(2,1)} %param.23), calls=%async_computation.2 | async-start | bytes 3145728 | tf_op jit(solution)/shard_map/all_to_all | solution.py:237
  59.4 147.3 %all-gather.12.cloned.1.call-start = ((), (), s32[]{:S(2)}) async-start(), calls=%async_computation.10 | async-start | bytes 10616832 | tf_op jit(solution)/shard_map/all_gather | solution.py:257
  62.7 449.4 %reduce-scatter.3.cloned.1.call-start = ((), (), s32[]{:S(2)}) async-start(), calls=%async_computation.6 | async-start | bytes 9400320 | tf_op jit(solution)/shard_map/reduce_scatter | solution.py:332
  62.8 33.0 %copy-start.85 = (s32[4]{0:T(128)}, s32[4]{0:T(128)S(1)}, u32[]{:S(2)}) copy-start(s32[4]{0:T(128)S(1)} %dynamic-slice_bitcast_fusion) | copy-start | bytes 52
  101.0 168.2 %copy-start.70 = (f32[768]{0:T(1024)}, f32[768]{0:T(1024)S(1)}, u32[]{:S(2)}) copy-start(f32[768]{0:T(1024)S(1)} %mul.222) | copy-start | bytes 9220
  129.3 39.3 %copy-start.22 = (bf16[256,768]{0,1:T(8,128)(2,1)}, bf16[256,768]{0,1:T(8,128)(2,1)S(1)}, u32[]{:S(2)}) copy-start(bf16[256,768]{0,1:T(8,128)(2,1)S(1)} %get-tuple-element.65) | copy-start | bytes 1179652
  204.5 64.7 %copy-start.65 = (f32[1024]{0:T(1024)}, f32[1024]{0:T(1024)S(1)}, u32[]{:S(2)}) copy-start(f32[1024]{0:T(1024)S(1)} %broadcast_multiply_fusion.4) | copy-start | bytes 12292
  206.6 62.6 %copy-start.72 = (f32[1024]{0:T(1024)}, f32[1024]{0:T(1024)S(1)}, u32[]{:S(2)}) copy-start(f32[1024]{0:T(1024)S(1)} %add_rsqrt_fusion.1) | copy-start | bytes 12292
  244.4 15.3 %copy-start.52 = (bf16[8,96,768]{2,1,0:T(8,128)(2,1)S(1)}, bf16[8,96,768]{2,1,0:T(8,128)(2,1)}, u32[]{:S(2)}) copy-start(bf16[8,96,768]{2,1,0:T(8,128)(2,1)} %get-tuple-element.53) | copy-start | bytes 3538948
  244.4 15.3 %copy-start.53 = (bf16[8,96,768]{2,1,0:T(8,128)(2,1)S(1)}, bf16[8,96,768]{2,1,0:T(8,128)(2,1)}, u32[]{:S(2)}) copy-start(bf16[8,96,768]{2,1,0:T(8,128)(2,1)} %get-tuple-element.54) | copy-start | bytes 3538948
  244.4 15.3 %copy-start.54 = (bf16[8,96,768]{2,1,0:T(8,128)(2,1)S(1)}, bf16[8,96,768]{2,1,0:T(8,128)(2,1)}, u32[]{:S(2)}) copy-start(bf16[8,96,768]{2,1,0:T(8,128)(2,1)} %get-tuple-element.55) | copy-start | bytes 3538948
  244.4 15.3 %copy-start.55 = (bf16[8,96,768]{2,1,0:T(8,128)(2,1)S(1)}, bf16[8,96,768]{2,1,0:T(8,128)(2,1)}, u32[]{:S(2)}) copy-start(bf16[8,96,768]{2,1,0:T(8,128)(2,1)} %get-tuple-element.56) | copy-start | bytes 3538948
  276.0 34.6 %copy-start.38 = (bf16[1024,12,64]{0,2,1:T(8,128)(2,1)}, bf16[1024,12,64]{0,2,1:T(8,128)(2,1)S(1)}, u32[]{:S(2)}) copy-start(bf16[1024,12,64]{0,2,1:T(8,128)(2,1)S(1)} %multiply_convert_fusion.5) | copy-start | bytes 4718596
  282.8 16.2 %slice-start.9 = ((s8[12582912]{0:T(1024)(128)(4,1)}), s8[4194304]{0:T(1024)(128)(4,1)S(1)}, s32[]{:S(2)}) async-start(s8[12582912]{0:T(1024)(128)(4,1)} %bitcast.289), calls=%async_computation.21 | async-start | bytes 8388608
  282.8 16.2 %slice-start.10 = ((s8[12582912]{0:T(1024)(128)(4,1)}), s8[4194304]{0:T(1024)(128)(4,1)S(1)}, s32[]{:S(2)}) async-start(s8[12582912]{0:T(1024)(128)(4,1)} %bitcast.289), calls=%async_computation.22 | async-start | bytes 8388608
  344.8 33.3 %copy-start.26 = (bf16[12,64,256]{2,1,0:T(8,128)(2,1)}, bf16[12,64,256]{2,1,0:T(8,128)(2,1)S(1)}, u32[]{:S(2)}) copy-start(bf16[12,64,256]{2,1,0:T(8,128)(2,1)S(1)} %convolution_convert_fusion.16) | copy-start | bytes 1179652
  441.6 150.8 %reduce-scatter.5.cloned.1.call-start = ((), (), s32[]{:S(2)}) async-start(), calls=%async_computation.8 | async-start | bytes 10616832 | tf_op jit(solution)/shard_map/reduce_scatter | solution.py:332
  480.6 111.8 %copy-start.61 = (bf16[4,12,64]{2,1,0:T(8,128)(2,1)S(1)}, bf16[4,12,64]{2,1,0:T(8,128)(2,1)}, u32[]{:S(2)}) copy-start(bf16[4,12,64]{2,1,0:T(8,128)(2,1)} %copy.106) | copy-start | bytes 18436
  480.6 301.5 %all-gather.8.cloned.1.call-start = ((), (), s32[]{:S(2)}) async-start(), calls=%async_computation.7 | async-start | bytes 5222400 | tf_op jit(solution)/shard_map/all_gather | solution.py:17
  512.2 306.0 %all-gather.10.cloned.1.call-start = ((), (), s32[]{:S(2)}) async-start(), calls=%async_computation.9 | async-start | bytes 5898240 | tf_op jit(solution)/shard_map/all_gather | solution.py:17
  616.1 83.5 %all-to-all-start.1 = ((bf16[4,2,98304]{2,1,0:T(2,128)(2,1)}), bf16[4,2,98304]{2,1,0:T(2,128)(2,1)}, u32[]{:S(2)}, u32[]{:S(2)}) async-start(bf16[4,2,98304]{2,1,0:T(2,128)(2,1)} %reshape.661), calls=%async_computation.1 | async-start | bytes 3145728 | tf_op jit(solution)/shard_map/all_to_all | solution.py:240
  699.6 78.1 %all-to-all-start.3 = ((bf16[4,2,98304]{2,1,0:T(2,128)(2,1)}), bf16[4,2,98304]{2,1,0:T(2,128)(2,1)}, u32[]{:S(2)}, u32[]{:S(2)}) async-start(bf16[4,2,98304]{2,1,0:T(2,128)(2,1)} %reshape.663), calls=%async_computation.3 | async-start | bytes 3145728 | tf_op jit(solution)/shard_map/all_to_all | solution.py:240
  (112 other events, 499.5 us)
Sparse Core Ops, SparseCore 0:
  12.8 56.9 all-gather.13
  72.3 58.8 all-gather.11
  441.7 70.3 reduce-scatter.2
  515.9 76.4 reduce-scatter.4
  593.9 113.8 all-gather.7
  709.3 108.8 all-gather.9
